TPU v7x, 32 devices: a whole 2x2x4 slice. The times are simulated.
32 devices in a mesh: groups: 2 (over x), lon: 16 (over z, y, core).
Axes of the slice: x: 2, y: 2, z: 4, core: 2. Of those that a mesh axis runs over, the one named last changes fastest.
Arguments:
- input_field: bfloat16 [96, 512, 512], P('groups', 'lon'), parts along dimension 0, may hold values from -8 to 8
- expand_weight: bfloat16 [512, 2048], replicated, may hold values from -0.25 to 0.25
- expand_bias: float32 [2048], replicated, may hold values from -3 to 3
- depth_weight: float32 [9, 2048], replicated, may hold values from -2 to 2
- depth_bias: float32 [2048], replicated, may hold values from -3 to 3
- squeeze_down: bfloat16 [2048, 128], replicated, may hold values from -0.125 to 0.125
- squeeze_up: bfloat16 [128, 2048], replicated, may hold values from -3 to 3
- project_weight: bfloat16 [2048, 512], replicated, may hold values from -0.125 to 0.125
- block_gain: float32 [512], replicated, may hold values from 0.1 to 1.9
- block_in_weight: bfloat16 [512, 1536], replicated, may hold values from -4 to 4
- block_out_weight: bfloat16 [512, 512], replicated, may hold values from -0.25 to 0.25
- block_table: float32 [225, 16], replicated, may hold values from -5 to 5
- grid_gain: float32 [512], replicated, may hold values from 0.1 to 1.9
- grid_in_weight: bfloat16 [512, 1536], replicated, may hold values from -4 to 4
- grid_out_weight: bfloat16 [512, 512], replicated, may hold values from -0.25 to 0.25
- grid_table: float32 [225, 16], replicated, may hold values from -5 to 5
Outputs:
- output_field: bfloat16 [96, 512, 512], P('groups', 'lon'), parts along dimension 0
There are 2 independent parts, one for each index of `groups`. A program takes and returns all parts, laid end to end along the dimension named above; an argument that names none is the same for every part. Nothing has to cross between parts.
All inputs are finite; a program needn't handle non-finite values.
Results may differ from a plain program's by a relative error of at most 0.012.
Values may be sent and summed in bfloat16 or wider, within the bound.
No kernel may reach another device: no remote copies, remote signals or barrier semaphores. Data moves between devices by JAX's collectives and lax.ppermute only.
A program may use at most 128 MiB of HBM per device.

v0:
```python
import jax
import jax.numpy as jnp
from jax import lax
from jax.sharding import PartitionSpec as P

HEADS = 16
HEAD_DIM = 32


def extended(cells, sides, width):
    for axis, dim in sides:
        count = lax.axis_size(axis)
        head = lax.slice_in_dim(cells, 0, width, axis=dim)
        tail = lax.slice_in_dim(cells, cells.shape[dim] - width, cells.shape[dim], axis=dim)
        cells = jnp.concatenate(
            [
                lax.ppermute(tail, axis, [(i, (i + 1) % count) for i in range(count)]),
                cells,
                lax.ppermute(head, axis, [((i + 1) % count, i) for i in range(count)]),
            ],
            axis=dim,
        )
    return cells


def relative_bias(pos_table):
    position = jnp.arange(64)
    win_row = position // 8
    win_col = position % 8
    rel_index = (win_row[:, None] - win_row[None, :] + 7) * 15 + (
        win_col[:, None] - win_col[None, :] + 7
    )
    one_hot = (rel_index[:, :, None] == jnp.arange(225)[None, None, :]).astype(jnp.float32)
    return jnp.einsum("ijr,rh->hij", one_hot, pos_table, precision=lax.Precision.HIGHEST)


def layer_normed(stream, gain):
    widened = stream.astype(jnp.float32)
    average = jnp.mean(widened, axis=-1, keepdims=True)
    centred = widened - average
    variance = jnp.mean(centred * centred, axis=-1, keepdims=True)
    return (centred * lax.rsqrt(variance + 1e-05) * gain).astype(jnp.bfloat16)


def attend_windows(mixed, rel_bias):
    scores = jnp.einsum(
        "nqhd,nkhd->nhqk", mixed[:, :, 0], mixed[:, :, 1], preferred_element_type=jnp.float32
    )
    scores = scores * HEAD_DIM ** (-0.5) + rel_bias[None]
    scores = scores - jnp.max(scores, axis=-1, keepdims=True)
    exponent = jnp.exp(scores)
    probabilities = (exponent / jnp.sum(exponent, axis=-1, keepdims=True)).astype(jnp.bfloat16)
    return jnp.einsum(
        "nhqk,nkhd->nqhd", probabilities, mixed[:, :, 2], preferred_element_type=jnp.float32
    ).astype(jnp.bfloat16)


def expand_cells(cells, expand_weight, expand_bias):
    row_count, col_count, channels = cells.shape
    hidden = (
        jnp.dot(cells.reshape(-1, channels), expand_weight, preferred_element_type=jnp.float32)
        + expand_bias
    )
    return (
        jax.nn.gelu(hidden, approximate=False)
        .astype(jnp.bfloat16)
        .reshape(row_count, col_count, -1)
    )


def mbconv_block(
    input_field,
    expand_weight,
    expand_bias,
    depth_weight,
    depth_bias,
    squeeze_down,
    squeeze_up,
    project_weight,
):
    row_count, col_count, channels = input_field.shape
    hidden = expand_cells(input_field, expand_weight, expand_bias)
    rimmed = extended(hidden, (("lon", 1),), 1)
    padded = jnp.pad(rimmed, ((1, 1), (0, 0), (0, 0)))
    summed = depth_bias + jnp.zeros((row_count, col_count, depth_bias.shape[0]), jnp.float32)
    for row_off in range(3):
        for col_off in range(3):
            summed = (
                summed
                + padded[row_off : row_off + row_count, col_off : col_off + col_count].astype(
                    jnp.float32
                )
                * depth_weight[row_off * 3 + col_off]
            )
    active = jax.nn.gelu(summed, approximate=False).astype(jnp.bfloat16)
    partial_sum = jnp.sum(active, axis=(0, 1), dtype=jnp.float32)
    pooled = lax.psum(partial_sum, "lon") / (row_count * col_count * lax.axis_size("lon"))
    squeezed = jax.nn.silu(
        jnp.dot(pooled, squeeze_down.astype(jnp.float32), precision=lax.Precision.HIGHEST)
    )
    gate_value = jax.nn.sigmoid(
        jnp.dot(squeezed, squeeze_up.astype(jnp.float32), precision=lax.Precision.HIGHEST)
    )
    gated_act = (active * gate_value).astype(jnp.bfloat16)
    result = jnp.dot(
        gated_act.reshape(-1, gated_act.shape[-1]),
        project_weight,
        preferred_element_type=jnp.float32,
    )
    result = result + input_field.reshape(-1, channels).astype(jnp.float32)
    return result.astype(jnp.bfloat16).reshape(row_count, col_count, channels)


def block_attention(stream, gain, in_weight, out_weight, pos_table):
    row_count, col_count, channels = stream.shape
    normed = layer_normed(stream, gain)
    mixed = jnp.dot(
        normed.reshape(-1, channels), in_weight, preferred_element_type=jnp.float32
    ).astype(jnp.bfloat16)
    mixed = mixed.reshape(row_count // 8, 8, col_count // 8, 8, 3 * channels).transpose(
        0, 2, 1, 3, 4
    )
    mixed = mixed.reshape(-1, 64, 3, HEADS, HEAD_DIM)
    heads_out = attend_windows(mixed, relative_bias(pos_table))
    heads_out = (
        heads_out.reshape(row_count // 8, col_count // 8, 8, 8, channels)
        .transpose(0, 2, 1, 3, 4)
        .reshape(-1, channels)
    )
    merged = jnp.dot(heads_out, out_weight, preferred_element_type=jnp.float32) + stream.reshape(
        -1, channels
    ).astype(jnp.float32)
    return merged.astype(jnp.bfloat16).reshape(row_count, col_count, channels)


def grid_windows(tensor):
    row_count, items, lon_count, channels = tensor.shape
    shaped = tensor.reshape(8, row_count // 8, items, 8, lon_count // 8, channels)
    return shaped.transpose(1, 2, 4, 0, 3, 5).reshape(-1, 64, channels)


def grid_restore(windows, row_count, items, lon_count):
    channels = windows.shape[-1]
    shaped = windows.reshape(row_count // 8, items, lon_count // 8, 8, 8, channels)
    return shaped.transpose(3, 0, 1, 4, 2, 5).reshape(row_count, items, lon_count, channels)


def grid_attend(mixed, rel_bias):
    row_count, items, lon_count, triple_width = mixed.shape
    windows = grid_windows(mixed).reshape(-1, 64, 3, HEADS, HEAD_DIM)
    heads_out = attend_windows(windows, rel_bias).reshape(-1, 64, triple_width // 3)
    return grid_restore(heads_out, row_count, items, lon_count)


def grid_attention(stream, gain, in_weight, out_weight, pos_table):
    row_count, col_count, channels = stream.shape
    lon_count = lax.axis_size("lon")
    items = col_count // lon_count
    rel_bias = relative_bias(pos_table)
    normed = layer_normed(stream, gain)
    mixed = jnp.dot(
        normed.reshape(-1, channels), in_weight, preferred_element_type=jnp.float32
    ).astype(jnp.bfloat16)
    mixed = mixed.reshape(row_count, items, lon_count, 3 * channels)
    heads_out = grid_attend(
        lax.all_to_all(mixed, "lon", split_axis=2, concat_axis=2, tiled=True), rel_bias
    )
    returned = lax.all_to_all(heads_out, "lon", split_axis=2, concat_axis=2, tiled=True)
    merged = jnp.dot(returned.reshape(-1, channels), out_weight, preferred_element_type=jnp.float32)
    merged = merged + stream.reshape(-1, channels).astype(jnp.float32)
    return merged.astype(jnp.bfloat16).reshape(row_count, col_count, channels)


def per_device(
    input_field,
    expand_weight,
    expand_bias,
    depth_weight,
    depth_bias,
    squeeze_down,
    squeeze_up,
    project_weight,
    block_gain,
    block_in_weight,
    block_out_weight,
    block_table,
    grid_gain,
    grid_in_weight,
    grid_out_weight,
    grid_table,
):
    first_stream = mbconv_block(
        input_field,
        expand_weight,
        expand_bias,
        depth_weight,
        depth_bias,
        squeeze_down,
        squeeze_up,
        project_weight,
    )
    second_stream = block_attention(
        first_stream, block_gain, block_in_weight, block_out_weight, block_table
    )
    return grid_attention(second_stream, grid_gain, grid_in_weight, grid_out_weight, grid_table)


def solution(mesh):
    return jax.shard_map(
        per_device,
        mesh=mesh,
        in_specs=(
            P("groups", "lon", None),
            P(),
            P(),
            P(),
            P(),
            P(),
            P(),
            P(),
            P(),
            P(),
            P(),
            P(),
            P(),
            P(),
            P(),
            P(),
        ),
        out_specs=P("groups", "lon", None),
        check_vma=False,
    )
```

profile of v0, /device:TPU:1, one launch (start us, length us, event | category | flops | bytes accessed | tf_op | source)
XLA Modules:
  0.0 534.6 jit_solution(4356687229449048533)
XLA Ops:
  1.6 30.8 %fusion.6 = bf16[1536,2048]{1,0:T(8,128)(2,1)S(1)} fusion(bf16[1536,512]{1,0:T(8,128)(2,1)} %bitcast.114, bf16[512,2048]{1,0:T(8,128)(2,1)S(1)} %copy-done, f32[2048]{0:T(1024)} %param.18), kind=kOutput, calls=%fused_computation.12 | convolution fusion | flops 3428843520 | bytes 9969664 | tf_op jit(solution)/shard_map/dot_general | solution.py:61
  56.3 48.9 %convert_reduce_fusion = (f32[2048]{0:T(1024)S(1)}, bf16[48,32,2048]{2,1,0:T(8,128)(2,1)}) fusion(f32[2048]{0:T(1024)S(1)} %bitcast.110, bf16[50,34,2048]{2,1,0:T(8,128)(2,1)S(1)} %fusion.30, f32[2048]{0:T(1024)S(1)} %bitcast.111, f32[2048]{0:T(1024)S(1)} %bitcast.104, f32[2048]{0:T(1024)S(1)} %bitcast.105, ...), kind=kLoop, calls=%fused_computation.8 | loop fusion | flops 314570752 | bytes 50814976 | tf_op jit(solution)/shard_map/reduce_sum | solution.py:96
  105.2 28.6 %psum.7 = f32[2048]{0:T(1024)S(1)} all-reduce(f32[2048]{0:T(1024)S(1)} %get-tuple-element.5), channel_id=1, replica_groups=mesh['groups'=2,'lon'=16] {'lon'}, use_global_device_ids=true, to_apply=%region_1.2 | all-reduce | flops 2048 | bytes 16384 | tf_op jit(solution)/shard_map/psum | solution.py:97
  150.9 21.1 %reshape.215 = bf16[24,64,3,16,32]{4,3,2,1,0:T(8,128)(2,1)} reshape(bf16[6,4,8,8,1536]{4,3,2,1,0:T(8,128)(2,1)} %bitcast.94) | data formatting | bytes 9437184 | tf_op jit(solution)/shard_map/reshape | solution.py:123
  172.0 14.3 %fusion.88 = (bf16[24,64,1,16,32]{4,3,2,1,0:T(8,128)(2,1)}, bf16[24,64,1,16,32]{4,3,2,1,0:T(8,128)(2,1)}, bf16[24,64,1,16,32]{4,3,2,1,0:T(8,128)(2,1)}) fusion(bf16[24,64,3,16,32]{4,3,2,1,0:T(8,128)(2,1)} %reshape.215), kind=kLoop, calls=%fused_computation.139 | loop fusion | bytes 9437184 | tf_op jit(solution)/shard_map/slice | solution.py:54
  186.4 8.0 %copy.79 = bf16[24,64,1,16,32]{1,4,3,0,2:T(8,128)(2,1)} copy(bf16[24,64,1,16,32]{4,3,2,1,0:T(8,128)(2,1)} %get-tuple-element.11) | data formatting | bytes 3145728
  194.4 8.0 %copy.80 = bf16[24,64,1,16,32]{1,4,3,0,2:T(8,128)(2,1)} copy(bf16[24,64,1,16,32]{4,3,2,1,0:T(8,128)(2,1)} %get-tuple-element.12) | data formatting | bytes 3145728
  202.4 8.0 %copy.78 = bf16[24,64,1,16,32]{1,4,3,0,2:T(8,128)(2,1)} copy(bf16[24,64,1,16,32]{4,3,2,1,0:T(8,128)(2,1)} %get-tuple-element.10) | data formatting | bytes 3145728
  215.1 8.3 %fusion.91 = (f32[24,16,64]{2,1,0:T(8,128)S(1)}, f32[24,16,64,64]{2,3,1,0:T(8,128)}) fusion(f32[24,16,64,64]{2,3,1,0:T(8,128)S(1)} %fusion.53, f32[16,64,64]{1,2,0:T(8,128)S(1)} %copy.58), kind=kOutput, calls=%fused_computation.142 | output fusion | flops 9437247 | bytes 12943360 | tf_op jit(solution)/shard_map/sub | solution.py:50
  223.4 9.0 %convert_bitcast_fusion.1 = bf16[24,64,16,32]{1,3,2,0:T(8,128)(2,1)} fusion(f32[24,16,64,64]{2,3,1,0:T(8,128)} %get-tuple-element.27, f32[24,16,64]{2,1,0:T(8,128)S(1)} %get-tuple-element.26, bf16[24,64,1,16,32]{1,4,3,0,2:T(8,128)(2,1)} %copy.78), kind=kOutput, calls=%fused_computation.100 | convolution fusion | flops 104595456 | bytes 9535488 | tf_op jit(solution)/shard_map/nhqk,nkhd->nqhd/dot_general | solution.py:53
  232.4 7.9 %copy.60 = bf16[24,64,16,32]{3,2,1,0:T(8,128)(2,1)} copy(bf16[24,64,16,32]{1,3,2,0:T(8,128)(2,1)} %convert_bitcast_fusion.1) | data formatting | bytes 3145728 | tf_op jit(solution)/shard_map/convert_element_type | solution.py:55
  240.3 8.4 %reshape.216 = bf16[6,4,8,8,512]{4,3,2,1,0:T(8,128)(2,1)S(1)} reshape(bf16[24,64,16,32]{3,2,1,0:T(8,128)(2,1)} %copy.60) | data formatting | bytes 3145728 | tf_op jit(solution)/shard_map/reshape | solution.py:126
  258.3 9.4 %copy.62 = bf16[48,2,16,1536]{3,1,0,2:T(2,128)(2,1)} copy(bf16[48,2,16,1536]{3,2,1,0:T(8,128)(2,1)} %bitcast.100) | data formatting | bytes 9437184 | tf_op jit(solution)/shard_map/reshape | solution.py:164
  279.1 83.6 %all-to-all-done = bf16[48,2,16,1536]{3,1,0,2:T(2,128)(2,1)} async-done(((bf16[48,2,16,1536]{3,1,0,2:T(2,128)(2,1)}), bf16[48,2,16,1536]{3,1,0,2:T(2,128)(2,1)}, u32[]{:S(2)}, u32[]{:S(2)}) %all-to-all-start) | async-done | bytes 4718624 | tf_op jit(solution)/shard_map/all_to_all | solution.py:166
  369.8 21.1 %reshape_reshape.6 = bf16[24,64,3,16,32]{4,3,2,1,0:T(8,128)(2,1)} reshape(bf16[6,2,2,8,8,1536]{5,4,3,2,1,0:T(8,128)(2,1)} %copy.64) | data formatting | bytes 9437184 | tf_op jit(solution)/shard_map/reshape;reshape | solution.py:150
  390.9 14.3 %fusion.87 = (bf16[24,64,1,16,32]{4,3,2,1,0:T(8,128)(2,1)}, bf16[24,64,1,16,32]{4,3,2,1,0:T(8,128)(2,1)}, bf16[24,64,1,16,32]{4,3,2,1,0:T(8,128)(2,1)}) fusion(bf16[24,64,3,16,32]{4,3,2,1,0:T(8,128)(2,1)} %reshape_reshape.6), kind=kLoop, calls=%fused_computation.138 | loop fusion | bytes 9437184 | tf_op jit(solution)/shard_map/slice | solution.py:54
  405.3 8.0 %copy.82 = bf16[24,64,1,16,32]{1,4,3,0,2:T(8,128)(2,1)} copy(bf16[24,64,1,16,32]{4,3,2,1,0:T(8,128)(2,1)} %get-tuple-element.8) | data formatting | bytes 3145728
  413.3 8.0 %copy.83 = bf16[24,64,1,16,32]{1,4,3,0,2:T(8,128)(2,1)} copy(bf16[24,64,1,16,32]{4,3,2,1,0:T(8,128)(2,1)} %get-tuple-element.9) | data formatting | bytes 3145728
  421.3 8.0 %copy.81 = bf16[24,64,1,16,32]{1,4,3,0,2:T(8,128)(2,1)} copy(bf16[24,64,1,16,32]{4,3,2,1,0:T(8,128)(2,1)} %get-tuple-element.7) | data formatting | bytes 3145728
  434.0 8.2 %fusion.92 = (f32[24,16,64]{2,1,0:T(8,128)S(1)}, f32[24,16,64,64]{2,3,1,0:T(8,128)}) fusion(f32[24,16,64,64]{2,3,1,0:T(8,128)S(1)} %fusion.49, f32[16,64,64]{1,2,0:T(8,128)S(1)} %copy.68), kind=kOutput, calls=%fused_computation.143 | output fusion | flops 9437247 | bytes 12943360 | tf_op jit(solution)/shard_map/sub | solution.py:50
  442.3 9.0 %convert_bitcast_fusion = bf16[24,64,16,32]{1,3,2,0:T(8,128)(2,1)} fusion(f32[24,16,64,64]{2,3,1,0:T(8,128)} %get-tuple-element.31, f32[24,16,64]{2,1,0:T(8,128)S(1)} %get-tuple-element.30, bf16[24,64,1,16,32]{1,4,3,0,2:T(8,128)(2,1)} %copy.81), kind=kOutput, calls=%fused_computation.99 | convolution fusion | flops 104595456 | bytes 9535488 | tf_op jit(solution)/shard_map/nhqk,nkhd->nqhd/dot_general | solution.py:53
  451.2 8.0 %copy.70 = bf16[24,64,16,32]{3,2,1,0:T(8,128)(2,1)} copy(bf16[24,64,16,32]{1,3,2,0:T(8,128)(2,1)} %convert_bitcast_fusion) | data formatting | bytes 3145728 | tf_op jit(solution)/shard_map/convert_element_type | solution.py:55
  459.3 9.3 %reshape_reshape.7 = bf16[6,2,2,8,8,512]{5,4,3,2,1,0:T(8,128)(2,1)} reshape(bf16[24,64,16,32]{3,2,1,0:T(8,128)(2,1)} %copy.70) | data formatting | bytes 3145728 | tf_op jit(solution)/shard_map/reshape;reshape | solution.py:144
  471.6 57.6 %all_to_all.10 = bf16[48,2,16,512]{3,1,0,2:T(2,128)(2,1)S(1)} all-to-all(bf16[48,2,16,512]{3,1,0,2:T(2,128)(2,1)S(1)} %bitcast.95), channel_id=1, replica_groups=mesh['groups'=2,'lon'=16] {'lon'}, dimensions={2} | all-to-all | bytes 3145728 | tf_op jit(solution)/shard_map/all_to_all | solution.py:168
  (71 shorter events, 88.1 us)
Async XLA Ops:
  0.0 1.6 copy-start
  1.6 36.8 %copy-start.7 = (f32[9,2048]{1,0:T(8,128)S(1)}, f32[9,2048]{1,0:T(8,128)}, u32[]{:S(2)}) copy-start(f32[9,2048]{1,0:T(8,128)} %param.19) | copy-start | bytes 221188
  1.6 37.0 %copy-start.13 = (f32[225,16]{0,1:T(8,128)S(1)}, f32[225,16]{0,1:T(8,128)}, u32[]{:S(2)}) copy-start(f32[225,16]{0,1:T(8,128)} %param.27) | copy-start | bytes 43204
  32.4 2.7 copy-start.2
  32.4 23.9 %copy-start.8 = (f32[2048]{0:T(1024)S(1)}, f32[2048]{0:T(1024)}, u32[]{:S(2)}) copy-start(f32[2048]{0:T(1024)} %param.20) | copy-start | bytes 24580
  35.7 11.6 %collective-permute-start = (bf16[48,1,2048]{2,1,0:T(2,128)(2,1)S(1)}, bf16[48,1,2048]{2,1,0:T(2,128)(2,1)S(1)}, u32[]{:S(2)}, u32[]{:S(2)}) collective-permute-start(bf16[48,1,2048]{2,1,0:T(2,128)(2,1)S(1)} %get-tuple-element.13), channel_id=1, source_target_pairs={{0,1},{1,2},{2,3},{3,4},{4,5},{5,6},{6,7},{7,8},{8,9},{9,10},{10,1... | collective-permute-start | bytes 589832 | tf_op jit(solution)/shard_map/ppermute | solution.py:17
  38.4 11.4 %collective-permute-start.1 = (bf16[48,1,2048]{2,1,0:T(2,128)(2,1)S(1)}, bf16[48,1,2048]{2,1,0:T(2,128)(2,1)S(1)}, u32[]{:S(2)}, u32[]{:S(2)}) collective-permute-start(bf16[48,1,2048]{2,1,0:T(2,128)(2,1)S(1)} %get-tuple-element.14), channel_id=1, source_target_pairs={{1,0},{2,1},{3,2},{4,3},{5,4},{6,5},{7,6},{8,7},{9,8},{10,9},{11,1... | collective-permute-start | bytes 589832 | tf_op jit(solution)/shard_map/ppermute | solution.py:19
  56.3 77.5 %copy-start.5 = (bf16[2048,128]{1,0:T(8,128)(2,1)S(1)}, bf16[2048,128]{1,0:T(8,128)(2,1)}, u32[]{:S(2)}) copy-start(bf16[2048,128]{1,0:T(8,128)(2,1)} %param.21) | copy-start | bytes 1572868
  56.3 77.8 %copy-start.6 = (bf16[128,2048]{1,0:T(8,128)(2,1)S(1)}, bf16[128,2048]{1,0:T(8,128)(2,1)}, u32[]{:S(2)}) copy-start(bf16[128,2048]{1,0:T(8,128)(2,1)} %param.22) | copy-start | bytes 1572868
  133.8 5.3 copy-start.9
  139.1 5.9 %copy-start.10 = (bf16[512,1536]{1,0:T(8,128)(2,1)S(1)}, bf16[512,1536]{1,0:T(8,128)(2,1)}, u32[]{:S(2)}) copy-start(bf16[512,1536]{1,0:T(8,128)(2,1)} %param.25) | copy-start | bytes 4718596
  139.1 5.9 %copy-start.15 = (f32[512]{0:T(512)S(1)}, f32[512]{0:T(512)}, u32[]{:S(2)}) copy-start(f32[512]{0:T(512)} %param.24) | copy-start | bytes 6148
  144.1 6.8 %copy-start.4 = (bf16[1536,512]{1,0:T(8,128)(2,1)}, bf16[1536,512]{1,0:T(8,128)(2,1)S(1)}, u32[]{:S(2)}) copy-start(bf16[1536,512]{1,0:T(8,128)(2,1)S(1)} %get-tuple-element.25) | copy-start | bytes 4718596
  232.4 16.5 %copy-start.11 = (bf16[512,512]{1,0:T(8,128)(2,1)S(1)}, bf16[512,512]{1,0:T(8,128)(2,1)}, u32[]{:S(2)}) copy-start(bf16[512,512]{1,0:T(8,128)(2,1)} %param.26) | copy-start | bytes 1572868
  232.4 19.9 %copy-start.16 = (f32[512]{0:T(512)S(1)}, f32[512]{0:T(512)}, u32[]{:S(2)}) copy-start(f32[512]{0:T(512)} %param.28) | copy-start | bytes 6148
  251.4 16.3 %copy-start.3 = (bf16[1536,512]{1,0:T(8,128)(2,1)}, bf16[1536,512]{1,0:T(8,128)(2,1)S(1)}, u32[]{:S(2)}) copy-start(bf16[1536,512]{1,0:T(8,128)(2,1)S(1)} %get-tuple-element.29) | copy-start | bytes 4718596
  258.3 17.3 %copy-start.14 = (f32[225,16]{0,1:T(8,128)S(1)}, f32[225,16]{0,1:T(8,128)}, u32[]{:S(2)}) copy-start(f32[225,16]{0,1:T(8,128)} %param.31) | copy-start | bytes 43204
  267.7 95.0 %all-to-all-start = ((bf16[48,2,16,1536]{3,1,0,2:T(2,128)(2,1)}), bf16[48,2,16,1536]{3,1,0,2:T(2,128)(2,1)}, u32[]{:S(2)}, u32[]{:S(2)}) async-start(bf16[48,2,16,1536]{3,1,0,2:T(2,128)(2,1)} %copy.62), calls=%async_computation | async-start | bytes 9437184 | tf_op jit(solution)/shard_map/all_to_all | solution.py:166
  451.2 79.6 %copy-start.12 = (bf16[512,512]{1,0:T(8,128)(2,1)S(1)}, bf16[512,512]{1,0:T(8,128)(2,1)}, u32[]{:S(2)}) copy-start(bf16[512,512]{1,0:T(8,128)(2,1)} %param.30) | copy-start | bytes 1572868
  451.2 83.2 %copy-start.1 = (bf16[512,2048]{1,0:T(8,128)(2,1)S(1)}, bf16[512,2048]{1,0:T(8,128)(2,1)}, u32[]{:S(2)}) copy-start(bf16[512,2048]{1,0:T(8,128)(2,1)} %param.17) | copy-start | bytes 6291460
where the time goes:
time: 544 us; the launch traced here: 535 us
  local copies, waits for them, and re-layouts  182 us (33%)
  waiting for transfers between devices  91.4 us (17%)
  blocking collectives  86.2 us (16%)
  matrix products  85.6 us (16%)
  other arithmetic  78.1 us (14%)
  starting transfers between devices  10.6 us (2%)
    all_to_all x1, waiting for transfers between devices, grid_attention(): lax.all_to_all(mixed, 'lon', split_axis=2, concat_axis=2, tiled=True)  83.6 us
    all_to_all x1, blocking collectives, grid_attention(): lax.all_to_all(heads_out, 'lon', split_axis=2, concat_axis=2, tiled=True)  57.6 us
    unnamed x40, local copies, waits for them, and re-layouts  52.4 us
    reduce_sum x1, other arithmetic, mbconv_block(): partial_sum = jnp.sum(active, axis=(0, 1), dtype=jnp.float32)  48.9 us
    dot_general x1, matrix products, expand_cells(): jnp.dot(cells.reshape(-1, channels), expand_weight, preferred_element_typ...  30.8 us
    slice x2, local copies, waits for them, and re-layouts, attend_windows(): mixed[:, :, 2]  28.7 us
    psum x1, blocking collectives, mbconv_block(): lax.psum(partial_sum, 'lon')  28.6 us
    reshape x1, local copies, waits for them, and re-layouts, block_attention(): mixed = mixed.reshape(-1, 64, 3, HEADS, HEAD_DIM)  21.1 us
  transfers between devices with their start and end apart: 3, of which 3 were waited for; matrix products, arithmetic and copies ran while one was open for 1% of the time, Pallas kernels for 0%

commit v1 on v0

--- a/solution.py
+++ b/solution.py
@@ -5,6 +5,29 @@
 
 HEADS = 16
 HEAD_DIM = 32
+
+
+def split_up(shard, dim, count):
+    shape = shard.shape
+    blocks = shard.reshape(*shape[:dim], count, shape[dim] // count, *shape[dim + 1 :])
+    return jnp.moveaxis(blocks, dim, 0)
+
+
+def joined_along(blocks, dim):
+    blocks = jnp.moveaxis(blocks, 0, dim)
+    shape = blocks.shape
+    return blocks.reshape(*shape[:dim], shape[dim] * shape[dim + 1], *shape[dim + 2 :])
+
+
+def exchange_in_pairs(shard, axis, split_dim, concat_dim):
+    size, place = (lax.axis_size(axis), lax.axis_index(axis))
+    parts = split_up(shard, split_dim, size)
+    finished = [parts[place]]
+    for lap in range(1, size):
+        sent = parts[place ^ lap]
+        finished.append(lax.ppermute(sent, axis, [(i, i ^ lap) for i in range(size)]))
+    parts = jnp.stack(finished)[place ^ jnp.arange(size)]
+    return joined_along(parts, concat_dim)
 
 
 def extended(cells, sides, width):
@@ -162,9 +185,7 @@
         normed.reshape(-1, channels), in_weight, preferred_element_type=jnp.float32
     ).astype(jnp.bfloat16)
     mixed = mixed.reshape(row_count, items, lon_count, 3 * channels)
-    heads_out = grid_attend(
-        lax.all_to_all(mixed, "lon", split_axis=2, concat_axis=2, tiled=True), rel_bias
-    )
+    heads_out = grid_attend(exchange_in_pairs(mixed, "lon", 2, 2), rel_bias)
     returned = lax.all_to_all(heads_out, "lon", split_axis=2, concat_axis=2, tiled=True)
     merged = jnp.dot(returned.reshape(-1, channels), out_weight, preferred_element_type=jnp.float32)
     merged = merged + stream.reshape(-1, channels).astype(jnp.float32)

time: 544 us -> 572 us (1.051)
  local copies, waits for them, and re-layouts: 182 us -> 214 us
  waiting for transfers between devices: 91.4 us -> 74.4 us
  starting transfers between devices: 10.6 us -> 20 us
    all_to_all x1 -> x0, waiting for transfers between devices: 83.6 us -> none  [grid_attention(): lax.all_to_all(mixed, 'lon', split_axis=2, concat_axis=2, tiled=True)]
    ppermute x0 -> x15, waiting for transfers between devices: none -> 70.9 us  [exchange_in_pairs(): lax.ppermute(sent, axis, [(i, i ^ lap) for i in range(size)])]
    ppermute x0 -> x15, starting transfers between devices: none -> 17.3 us  [exchange_in_pairs(): lax.ppermute(sent, axis, [(i, i ^ lap) for i in range(size)])]
    another operation x0 -> x2, local copies, waits for them, and re-layouts: none -> 14 us
    unnamed x40 -> x72, local copies, waits for them, and re-layouts: 52.4 us -> 65.3 us
    transpose x0 -> x1, local copies, waits for them, and re-layouts: none -> 9.37 us  [joined_along(): blocks = jnp.moveaxis(blocks, 0, dim)]
    reshape x1 -> x0, local copies, waits for them, and re-layouts: 9.36 us -> none  [grid_attention(): mixed = mixed.reshape(row_count, items, lon_count, 3 * channels)]
    all_to_all x1 -> x0, starting transfers between devices: 7.92 us -> none  [grid_attention(): lax.all_to_all(mixed, 'lon', split_axis=2, concat_axis=2, tiled=True)]
  transfers between devices with their start and end apart: 3 -> 17, of which waited for: 3 -> 9; matrix products, arithmetic and copies ran while one was open for 1% -> 4% of each run, Pallas kernels for 0% -> 0%
where the time goes in v1:
time: 572 us; the launch traced here: 562 us
  local copies, waits for them, and re-layouts  214 us (37%)
  blocking collectives  90.2 us (16%)
  matrix products  84.2 us (15%)
  other arithmetic  78.2 us (14%)
  waiting for transfers between devices  74.4 us (13%)
  starting transfers between devices  20 us (3%)
    ppermute x15, waiting for transfers between devices, exchange_in_pairs(): lax.ppermute(sent, axis, [(i, i ^ lap) for i in range(size)])  70.9 us
    unnamed x72, local copies, waits for them, and re-layouts  65.3 us
    all_to_all x1, blocking collectives, grid_attention(): lax.all_to_all(heads_out, 'lon', split_axis=2, concat_axis=2, tiled=True)  61.2 us
    reduce_sum x1, other arithmetic, mbconv_block(): partial_sum = jnp.sum(active, axis=(0, 1), dtype=jnp.float32)  48.9 us
    dot_general x1, matrix products, expand_cells(): jnp.dot(cells.reshape(-1, channels), expand_weight, preferred_element_typ...  30.8 us
    psum x1, blocking collectives, mbconv_block(): lax.psum(partial_sum, 'lon')  29 us
    slice x2, local copies, waits for them, and re-layouts, attend_windows(): mixed[:, :, 2]  28.5 us
    reshape x1, local copies, waits for them, and re-layouts, block_attention(): mixed = mixed.reshape(-1, 64, 3, HEADS, HEAD_DIM)  21.1 us
  transfers between devices with their start and end apart: 17, of which 9 were waited for; matrix products, arithmetic and copies ran while one was open for 4% of the time, Pallas kernels for 0%

profile of v1, /device:TPU:1, one launch (start us, length us, event | category | flops | bytes accessed | tf_op | source)
XLA Modules:
  0.0 561.8 jit_solution(14116750661190454981)
XLA Ops:
  1.6 30.8 %fusion.6 = bf16[1536,2048]{1,0:T(8,128)(2,1)S(1)} fusion(bf16[1536,512]{1,0:T(8,128)(2,1)} %bitcast.246, bf16[512,2048]{1,0:T(8,128)(2,1)S(1)} %copy-done, f32[2048]{0:T(1024)} %param.18), kind=kOutput, calls=%fused_computation.13 | convolution fusion | flops 3428843520 | bytes 9969664 | tf_op jit(solution)/shard_map/dot_general | solution.py:84
  56.3 48.9 %convert_reduce_fusion = (f32[2048]{0:T(1024)S(1)}, bf16[48,32,2048]{2,1,0:T(8,128)(2,1)}) fusion(f32[2048]{0:T(1024)S(1)} %bitcast.242, bf16[50,34,2048]{2,1,0:T(8,128)(2,1)S(1)} %fusion.30, f32[2048]{0:T(1024)S(1)} %bitcast.243, f32[2048]{0:T(1024)S(1)} %bitcast.236, f32[2048]{0:T(1024)S(1)} %bitcast.237, ...), kind=kLoop, calls=%fused_computation.9 | loop fusion | flops 314570752 | bytes 50814976 | tf_op jit(solution)/shard_map/reduce_sum | solution.py:119
  105.2 29.0 %psum.7 = f32[2048]{0:T(1024)S(1)} all-reduce(f32[2048]{0:T(1024)S(1)} %get-tuple-element.5), channel_id=1, replica_groups=mesh['groups'=2,'lon'=16] {'lon'}, use_global_device_ids=true, to_apply=%region_1.2 | all-reduce | flops 2048 | bytes 16384 | tf_op jit(solution)/shard_map/psum | solution.py:120
  151.4 21.1 %reshape.256 = bf16[24,64,3,16,32]{4,3,2,1,0:T(8,128)(2,1)} reshape(bf16[6,4,8,8,1536]{4,3,2,1,0:T(8,128)(2,1)} %bitcast.212) | data formatting | bytes 9437184 | tf_op jit(solution)/shard_map/reshape | solution.py:146
  172.6 14.3 %fusion.90 = (bf16[24,64,1,16,32]{4,3,2,1,0:T(8,128)(2,1)}, bf16[24,64,1,16,32]{4,3,2,1,0:T(8,128)(2,1)}, bf16[24,64,1,16,32]{4,3,2,1,0:T(8,128)(2,1)}) fusion(bf16[24,64,3,16,32]{4,3,2,1,0:T(8,128)(2,1)} %reshape.256), kind=kLoop, calls=%fused_computation.191 | loop fusion | bytes 9437184 | tf_op jit(solution)/shard_map/slice | solution.py:77
  194.8 8.0 %copy.172 = bf16[24,64,1,16,32]{1,4,3,0,2:T(8,128)(2,1)} copy(bf16[24,64,1,16,32]{4,3,2,1,0:T(8,128)(2,1)} %get-tuple-element.12) | data formatting | bytes 3145728
  202.9 8.0 %copy.170 = bf16[24,64,1,16,32]{1,4,3,0,2:T(8,128)(2,1)} copy(bf16[24,64,1,16,32]{4,3,2,1,0:T(8,128)(2,1)} %get-tuple-element.10) | data formatting | bytes 3145728
  215.6 8.5 %fusion.93 = (f32[24,16,64]{2,1,0:T(8,128)S(1)}, f32[24,16,64,64]{2,3,1,0:T(8,128)}) fusion(f32[24,16,64,64]{2,3,1,0:T(8,128)S(1)} %fusion.53, f32[16,64,64]{1,2,0:T(8,128)S(1)} %copy.121), kind=kOutput, calls=%fused_computation.194 | output fusion | flops 9437247 | bytes 12943360 | tf_op jit(solution)/shard_map/sub | solution.py:73
  224.1 8.9 %convert_bitcast_fusion.1 = bf16[24,64,16,32]{1,3,2,0:T(8,128)(2,1)} fusion(f32[24,16,64,64]{2,3,1,0:T(8,128)} %get-tuple-element.43, f32[24,16,64]{2,1,0:T(8,128)S(1)} %get-tuple-element.42, bf16[24,64,1,16,32]{1,4,3,0,2:T(8,128)(2,1)} %copy.170), kind=kOutput, calls=%fused_computation.101 | convolution fusion | flops 104595456 | bytes 9535488 | tf_op jit(solution)/shard_map/nhqk,nkhd->nqhd/dot_general | solution.py:76
  241.0 8.4 %reshape.257 = bf16[6,4,8,8,512]{4,3,2,1,0:T(8,128)(2,1)S(1)} reshape(bf16[24,64,16,32]{3,2,1,0:T(8,128)(2,1)} %copy.123) | data formatting | bytes 3145728 | tf_op jit(solution)/shard_map/reshape | solution.py:149
  257.6 13.2 %constant_dynamic-slice_fusion = (bf16[48,2,1,1,1536]{4,2,1,0,3:T(2,128)(2,1)S(1)}, bf16[48,2,1,1,1536]{4,2,1,0,3:T(2,128)(2,1)S(1)}, bf16[48,2,1,1,1536]{4,2,1,...) fusion(bf16[48,2,16,1,1536]{4,2,1,0,3:T(8,128)(2,1)S(1)} %bitca, ...), kind=kLoop, calls=%fused_computation.155 | loop fusion | bytes 9437248 | tf_op jit(solution)/shard_map/dynamic-slice.15
  294.0 11.7 %collective-permute-done.7 = bf16[48,2,1,1536]{3,0,1,2:T(8,128)(2,1)S(1)} collective-permute-done((bf16[48,2,1,1536]{3,0,1,2:T(8,128)(2,1)S(1)}, bf16[48,2,1,1536]{3,0,1,2:T(8,128)(2,1)S(1)}, u32[]{:S(2)}, u32[]{:S(2)}) %collective-permute-start.7) | collective-permute-done | bytes 294944 | tf_op jit(solution)/shard_map/ppermute | solution.py:28
  318.4 25.4 %collective-permute-done.10 = bf16[48,2,1,1536]{3,0,1,2:T(8,128)(2,1)S(1)} collective-permute-done((bf16[48,2,1,1536]{3,0,1,2:T(8,128)(2,1)S(1)}, bf16[48,2,1,1536]{3,0,1,2:T(8,128)(2,1)S(1)}, u32[]{:S(2)}, u32[]{:S(2)}) %collective-permute-start.10) | collective-permute-done | bytes 294944 | tf_op jit(solution)/shard_map/ppermute | solution.py:28
  349.8 18.9 %collective-permute-done.12 = bf16[48,2,1,1536]{3,0,1,2:T(8,128)(2,1)S(1)} collective-permute-done((bf16[48,2,1,1536]{3,0,1,2:T(8,128)(2,1)S(1)}, bf16[48,2,1,1536]{3,0,1,2:T(8,128)(2,1)S(1)}, u32[]{:S(2)}, u32[]{:S(2)}) %collective-permute-start.12) | collective-permute-done | bytes 294944 | tf_op jit(solution)/shard_map/ppermute | solution.py:28
  377.9 9.4 %copy.156 = bf16[48,2,16,1,1536]{4,1,2,0,3:T(2,128)(2,1)} copy(bf16[48,2,16,1,1536]{4,0,1,2,3:T(8,128)(2,1)} %bitcast.210) | data formatting | bytes 9437184 | tf_op jit(solution)/shard_map/transpose | solution.py:17
  392.9 21.1 %reshape_reshape.14 = bf16[24,64,3,16,32]{4,3,2,1,0:T(8,128)(2,1)} reshape(bf16[6,2,2,8,8,1536]{5,4,3,2,1,0:T(8,128)(2,1)} %copy.157) | data formatting | bytes 9437184 | tf_op jit(solution)/shard_map/reshape;reshape | solution.py:173
  414.0 14.3 %fusion.89 = (bf16[24,64,1,16,32]{4,3,2,1,0:T(8,128)(2,1)}, bf16[24,64,1,16,32]{4,3,2,1,0:T(8,128)(2,1)}, bf16[24,64,1,16,32]{4,3,2,1,0:T(8,128)(2,1)}) fusion(bf16[24,64,3,16,32]{4,3,2,1,0:T(8,128)(2,1)} %reshape_reshape.14), kind=kLoop, calls=%fused_computation.190 | loop fusion | bytes 9437184 | tf_op jit(solution)/shard_map/slice | solution.py:77
  428.3 8.2 %copy.190 = bf16[24,64,1,16,32]{1,4,3,0,2:T(8,128)(2,1)} copy(bf16[24,64,1,16,32]{4,3,2,1,0:T(8,128)(2,1)} %get-tuple-element.8) | data formatting | bytes 3145728
  444.5 8.1 %copy.189 = bf16[24,64,1,16,32]{1,4,3,0,2:T(8,128)(2,1)} copy(bf16[24,64,1,16,32]{4,3,2,1,0:T(8,128)(2,1)} %get-tuple-element.7) | data formatting | bytes 3145728
  457.3 8.1 %fusion.94 = (f32[24,16,64]{2,1,0:T(8,128)S(1)}, f32[24,16,64,64]{2,3,1,0:T(8,128)}) fusion(f32[24,16,64,64]{2,3,1,0:T(8,128)S(1)} %fusion.49, f32[16,64,64]{1,2,0:T(8,128)S(1)} %copy-done.3), kind=kOutput, calls=%fused_computation.195 | output fusion | flops 9437247 | bytes 12943360 | tf_op jit(solution)/shard_map/sub | solution.py:73
  465.4 8.9 %convert_bitcast_fusion = bf16[24,64,16,32]{1,3,2,0:T(8,128)(2,1)} fusion(f32[24,16,64,64]{2,3,1,0:T(8,128)} %get-tuple-element.47, f32[24,16,64]{2,1,0:T(8,128)S(1)} %get-tuple-element.46, bf16[24,64,1,16,32]{1,4,3,0,2:T(8,128)(2,1)} %copy.189), kind=kOutput, calls=%fused_computation.100 | convolution fusion | flops 104595456 | bytes 9535488 | tf_op jit(solution)/shard_map/nhqk,nkhd->nqhd/dot_general | solution.py:76
  474.4 8.0 %copy.163 = bf16[24,64,16,32]{3,2,1,0:T(8,128)(2,1)} copy(bf16[24,64,16,32]{1,3,2,0:T(8,128)(2,1)} %convert_bitcast_fusion) | data formatting | bytes 3145728 | tf_op jit(solution)/shard_map/convert_element_type | solution.py:78
  482.4 9.5 %reshape_reshape.15 = bf16[6,2,2,8,8,512]{5,4,3,2,1,0:T(8,128)(2,1)} reshape(bf16[24,64,16,32]{3,2,1,0:T(8,128)(2,1)} %copy.163) | data formatting | bytes 3145728 | tf_op jit(solution)/shard_map/reshape;reshape | solution.py:167
  495.0 61.2 %all_to_all.5 = bf16[48,2,16,512]{3,1,0,2:T(2,128)(2,1)S(1)} all-to-all(bf16[48,2,16,512]{3,1,0,2:T(2,128)(2,1)S(1)} %bitcast.213), channel_id=1, replica_groups=mesh['groups'=2,'lon'=16] {'lon'}, dimensions={2} | all-to-all | bytes 3145728 | tf_op jit(solution)/shard_map/all_to_all | solution.py:189
  (136 shorter events, 148.8 us)
Async XLA Ops:
  1.6 36.9 %copy-start.8 = (f32[9,2048]{1,0:T(8,128)S(1)}, f32[9,2048]{1,0:T(8,128)}, u32[]{:S(2)}) copy-start(f32[9,2048]{1,0:T(8,128)} %param.19) | copy-start | bytes 221188
  1.6 37.0 %copy-start.14 = (f32[225,16]{0,1:T(8,128)S(1)}, f32[225,16]{0,1:T(8,128)}, u32[]{:S(2)}) copy-start(f32[225,16]{0,1:T(8,128)} %param.27) | copy-start | bytes 43204
  1.6 40.5 %copy-start.15 = (f32[225,16]{0,1:T(8,128)S(1)}, f32[225,16]{0,1:T(8,128)}, u32[]{:S(2)}) copy-start(f32[225,16]{0,1:T(8,128)} %param.31) | copy-start | bytes 43204
  35.8 11.6 %collective-permute-start = (bf16[48,1,2048]{2,1,0:T(2,128)(2,1)S(1)}, bf16[48,1,2048]{2,1,0:T(2,128)(2,1)S(1)}, u32[]{:S(2)}, u32[]{:S(2)}) collective-permute-start(bf16[48,1,2048]{2,1,0:T(2,128)(2,1)S(1)} %get-tuple-element.13), channel_id=1, source_target_pairs={{0,1},{1,2},{2,3},{3,4},{4,5},{5,6},{6,7},{7,8},{8,9},{9,10},{10,1... | collective-permute-start | bytes 589832 | tf_op jit(solution)/shard_map/ppermute | solution.py:40
  38.4 11.4 %collective-permute-start.1 = (bf16[48,1,2048]{2,1,0:T(2,128)(2,1)S(1)}, bf16[48,1,2048]{2,1,0:T(2,128)(2,1)S(1)}, u32[]{:S(2)}, u32[]{:S(2)}) collective-permute-start(bf16[48,1,2048]{2,1,0:T(2,128)(2,1)S(1)} %get-tuple-element.14), channel_id=1, source_target_pairs={{1,0},{2,1},{3,2},{4,3},{5,4},{6,5},{7,6},{8,7},{9,8},{10,9},{11,1... | collective-permute-start | bytes 589832 | tf_op jit(solution)/shard_map/ppermute | solution.py:42
  56.3 78.0 %copy-start.6 = (bf16[2048,128]{1,0:T(8,128)(2,1)S(1)}, bf16[2048,128]{1,0:T(8,128)(2,1)}, u32[]{:S(2)}) copy-start(bf16[2048,128]{1,0:T(8,128)(2,1)} %param.21) | copy-start | bytes 1572868
  56.3 78.3 %copy-start.7 = (bf16[128,2048]{1,0:T(8,128)(2,1)S(1)}, bf16[128,2048]{1,0:T(8,128)(2,1)}, u32[]{:S(2)}) copy-start(bf16[128,2048]{1,0:T(8,128)(2,1)} %param.22) | copy-start | bytes 1572868
  271.0 8.7 %collective-permute-start.2 = (bf16[48,2,1,1536]{3,0,1,2:T(8,128)(2,1)S(1)}, bf16[48,2,1,1536]{3,0,1,2:T(8,128)(2,1)S(1)}, u32[]{:S(2)}, u32[]{:S(2)}) collective-permute-start(bf16[48,2,1,1536]{3,0,1,2:T(8,128)(2,1)S(1)} %bitcast.234), channel_id=1, source_target_pairs={{0,1},{1,0},{2,3},{3,2},{4,5},{5,4},{6,7},{7,6},{8,9},{9,8},{10,11... | collective-permute-start | bytes 884744 | tf_op jit(solution)/shard_map/ppermute | solution.py:28
  273.8 8.7 %collective-permute-start.3 = (bf16[48,2,1,1536]{3,0,1,2:T(8,128)(2,1)S(1)}, bf16[48,2,1,1536]{3,0,1,2:T(8,128)(2,1)S(1)}, u32[]{:S(2)}, u32[]{:S(2)}) collective-permute-start(bf16[48,2,1,1536]{3,0,1,2:T(8,128)(2,1)S(1)} %bitcast.233), channel_id=1, source_target_pairs={{0,2},{1,3},{2,0},{3,1},{4,6},{5,7},{6,4},{7,5},{8,10},{9,11},{10,... | collective-permute-start | bytes 884744 | tf_op jit(solution)/shard_map/ppermute | solution.py:28
  274.0 15.2 %collective-permute-start.4 = (bf16[48,2,1,1536]{3,0,1,2:T(8,128)(2,1)S(1)}, bf16[48,2,1,1536]{3,0,1,2:T(8,128)(2,1)S(1)}, u32[]{:S(2)}, u32[]{:S(2)}) collective-permute-start(bf16[48,2,1,1536]{3,0,1,2:T(8,128)(2,1)S(1)} %bitcast.232), channel_id=1, source_target_pairs={{0,3},{1,2},{2,1},{3,0},{4,7},{5,6},{6,5},{7,4},{8,11},{9,10},{10,... | collective-permute-start | bytes 884744 | tf_op jit(solution)/shard_map/ppermute | solution.py:28
  275.8 14.2 %collective-permute-start.5 = (bf16[48,2,1,1536]{3,0,1,2:T(8,128)(2,1)S(1)}, bf16[48,2,1,1536]{3,0,1,2:T(8,128)(2,1)S(1)}, u32[]{:S(2)}, u32[]{:S(2)}) collective-permute-start(bf16[48,2,1,1536]{3,0,1,2:T(8,128)(2,1)S(1)} %bitcast.231), channel_id=1, source_target_pairs={{0,4},{1,5},{2,6},{3,7},{4,0},{5,1},{6,2},{7,3},{8,12},{9,13},{10,... | collective-permute-start | bytes 884744 | tf_op jit(solution)/shard_map/ppermute | solution.py:28
  276.0 17.2 %collective-permute-start.6 = (bf16[48,2,1,1536]{3,0,1,2:T(8,128)(2,1)S(1)}, bf16[48,2,1,1536]{3,0,1,2:T(8,128)(2,1)S(1)}, u32[]{:S(2)}, u32[]{:S(2)}) collective-permute-start(bf16[48,2,1,1536]{3,0,1,2:T(8,128)(2,1)S(1)} %bitcast.230), channel_id=1, source_target_pairs={{0,5},{1,4},{2,7},{3,6},{4,1},{5,0},{6,3},{7,2},{8,13},{9,12},{10,... | collective-permute-start | bytes 884744 | tf_op jit(solution)/shard_map/ppermute | solution.py:28
  279.7 25.9 %collective-permute-start.7 = (bf16[48,2,1,1536]{3,0,1,2:T(8,128)(2,1)S(1)}, bf16[48,2,1,1536]{3,0,1,2:T(8,128)(2,1)S(1)}, u32[]{:S(2)}, u32[]{:S(2)}) collective-permute-start(bf16[48,2,1,1536]{3,0,1,2:T(8,128)(2,1)S(1)} %bitcast.229), channel_id=1, source_target_pairs={{0,6},{1,7},{2,4},{3,5},{4,2},{5,3},{6,0},{7,1},{8,14},{9,15},{10,... | collective-permute-start | bytes 884744 | tf_op jit(solution)/shard_map/ppermute | solution.py:28
  282.5 30.3 %collective-permute-start.8 = (bf16[48,2,1,1536]{3,0,1,2:T(8,128)(2,1)S(1)}, bf16[48,2,1,1536]{3,0,1,2:T(8,128)(2,1)S(1)}, u32[]{:S(2)}, u32[]{:S(2)}) collective-permute-start(bf16[48,2,1,1536]{3,0,1,2:T(8,128)(2,1)S(1)} %bitcast.228), channel_id=1, source_target_pairs={{0,7},{1,6},{2,5},{3,4},{4,3},{5,2},{6,1},{7,0},{8,15},{9,14},{10,... | collective-permute-start | bytes 884744 | tf_op jit(solution)/shard_map/ppermute | solution.py:28
  289.2 28.3 %collective-permute-start.9 = (bf16[48,2,1,1536]{3,0,1,2:T(8,128)(2,1)S(1)}, bf16[48,2,1,1536]{3,0,1,2:T(8,128)(2,1)S(1)}, u32[]{:S(2)}, u32[]{:S(2)}) collective-permute-start(bf16[48,2,1,1536]{3,0,1,2:T(8,128)(2,1)S(1)} %bitcast.227), channel_id=1, source_target_pairs={{0,8},{1,9},{2,10},{3,11},{4,12},{5,13},{6,14},{7,15},{8,0},{9,1},... | collective-permute-start | bytes 884744 | tf_op jit(solution)/shard_map/ppermute | solution.py:28
  290.0 53.8 %collective-permute-start.10 = (bf16[48,2,1,1536]{3,0,1,2:T(8,128)(2,1)S(1)}, bf16[48,2,1,1536]{3,0,1,2:T(8,128)(2,1)S(1)}, u32[]{:S(2)}, u32[]{:S(2)}) collective-permute-start(bf16[48,2,1,1536]{3,0,1,2:T(8,128)(2,1)S(1)} %bitcast.226), channel_id=1, source_target_pairs={{0,9},{1,8},{2,11},{3,10},{4,13},{5,12},{6,15},{7,14},{8,1},{9,0},... | collective-permute-start | bytes 884744 | tf_op jit(solution)/shard_map/ppermute | solution.py:28
  293.2 55.7 %collective-permute-start.11 = (bf16[48,2,1,1536]{3,0,1,2:T(8,128)(2,1)S(1)}, bf16[48,2,1,1536]{3,0,1,2:T(8,128)(2,1)S(1)}, u32[]{:S(2)}, u32[]{:S(2)}) collective-permute-start(bf16[48,2,1,1536]{3,0,1,2:T(8,128)(2,1)S(1)} %bitcast.225), channel_id=1, source_target_pairs={{0,10},{1,11},{2,8},{3,9},{4,14},{5,15},{6,12},{7,13},{8,2},{9,3},... | collective-permute-start | bytes 884744 | tf_op jit(solution)/shard_map/ppermute | solution.py:28
  305.6 63.1 %collective-permute-start.12 = (bf16[48,2,1,1536]{3,0,1,2:T(8,128)(2,1)S(1)}, bf16[48,2,1,1536]{3,0,1,2:T(8,128)(2,1)S(1)}, u32[]{:S(2)}, u32[]{:S(2)}) collective-permute-start(bf16[48,2,1,1536]{3,0,1,2:T(8,128)(2,1)S(1)} %bitcast.224), channel_id=1, source_target_pairs={{0,11},{1,10},{2,9},{3,8},{4,15},{5,14},{6,13},{7,12},{8,3},{9,2},... | collective-permute-start | bytes 884744 | tf_op jit(solution)/shard_map/ppermute | solution.py:28
  312.8 56.8 %collective-permute-start.13 = (bf16[48,2,1,1536]{3,0,1,2:T(8,128)(2,1)S(1)}, bf16[48,2,1,1536]{3,0,1,2:T(8,128)(2,1)S(1)}, u32[]{:S(2)}, u32[]{:S(2)}) collective-permute-start(bf16[48,2,1,1536]{3,0,1,2:T(8,128)(2,1)S(1)} %bitcast.223), channel_id=1, source_target_pairs={{0,12},{1,13},{2,14},{3,15},{4,8},{5,9},{6,10},{7,11},{8,4},{9,5},... | collective-permute-start | bytes 884744 | tf_op jit(solution)/shard_map/ppermute | solution.py:28
  317.6 52.8 %collective-permute-start.14 = (bf16[48,2,1,1536]{3,0,1,2:T(8,128)(2,1)S(1)}, bf16[48,2,1,1536]{3,0,1,2:T(8,128)(2,1)S(1)}, u32[]{:S(2)}, u32[]{:S(2)}) collective-permute-start(bf16[48,2,1,1536]{3,0,1,2:T(8,128)(2,1)S(1)} %bitcast.222), channel_id=1, source_target_pairs={{0,13},{1,12},{2,15},{3,14},{4,9},{5,8},{6,11},{7,10},{8,5},{9,4},... | collective-permute-start | bytes 884744 | tf_op jit(solution)/shard_map/ppermute | solution.py:28
  343.8 27.3 %collective-permute-start.15 = (bf16[48,2,1,1536]{3,0,1,2:T(8,128)(2,1)S(1)}, bf16[48,2,1,1536]{3,0,1,2:T(8,128)(2,1)S(1)}, u32[]{:S(2)}, u32[]{:S(2)}) collective-permute-start(bf16[48,2,1,1536]{3,0,1,2:T(8,128)(2,1)S(1)} %bitcast.221), channel_id=1, source_target_pairs={{0,14},{1,15},{2,12},{3,13},{4,10},{5,11},{6,8},{7,9},{8,6},{9,7},... | collective-permute-start | bytes 884744 | tf_op jit(solution)/shard_map/ppermute | solution.py:28
  348.9 23.0 %collective-permute-start.16 = (bf16[48,2,1,1536]{3,0,1,2:T(8,128)(2,1)S(1)}, bf16[48,2,1,1536]{3,0,1,2:T(8,128)(2,1)S(1)}, u32[]{:S(2)}, u32[]{:S(2)}) collective-permute-start(bf16[48,2,1,1536]{3,0,1,2:T(8,128)(2,1)S(1)} %bitcast.220), channel_id=1, source_target_pairs={{0,15},{1,14},{2,13},{3,12},{4,11},{5,10},{6,9},{7,8},{8,7},{9,6},... | collective-permute-start | bytes 884744 | tf_op jit(solution)/shard_map/ppermute | solution.py:28
  474.4 83.4 %copy-start.13 = (bf16[512,512]{1,0:T(8,128)(2,1)S(1)}, bf16[512,512]{1,0:T(8,128)(2,1)}, u32[]{:S(2)}) copy-start(bf16[512,512]{1,0:T(8,128)(2,1)} %param.30) | copy-start | bytes 1572868
  474.4 87.0 %copy-start.1 = (bf16[512,2048]{1,0:T(8,128)(2,1)S(1)}, bf16[512,2048]{1,0:T(8,128)(2,1)}, u32[]{:S(2)}) copy-start(bf16[512,2048]{1,0:T(8,128)(2,1)} %param.17) | copy-start | bytes 6291460
  (11 other events, 106.7 us)
